TPU v7x, 512 devices: a whole 4x8x8 slice. The times are simulated.
512 devices in a mesh: dp: 4 (over x), expert: 128 (over z, y, core).
Axes of the slice: x: 4, y: 8, z: 8, core: 2. Of those that a mesh axis runs over, the one named last changes fastest.
Arguments:
- tokens: bfloat16 [8192, 2048], P(('dp', 'expert')), may hold values from -6 to 6
- cotangent: bfloat16 [8192, 2048], P(('dp', 'expert')), may hold values from -6 to 6
- routes: int32 [8192, 8], P(('dp', 'expert')), may hold values from 0 to 127, all different within a row; in each aligned block of 16 rows (0 to 15, 16 to 31, ...) at most 2 rows name the same one
- gate_values: float32 [8192, 8], P(('dp', 'expert')), may hold values from 0.1 to 1
- gate_weight: bfloat16 [128, 768, 2048], P('expert', 'dp'), may hold values from -0.125 to 0.125
- up_weight: bfloat16 [128, 768, 2048], P('expert', 'dp'), may hold values from -0.125 to 0.125
- down_weight: bfloat16 [128, 768, 2048], P('expert', None, 'dp'), may hold values from -0.21875 to 0.21875
Outputs:
- mixed: bfloat16 [8192, 2048], P(('dp', 'expert'))
- grad_gate_weight: bfloat16 [128, 768, 2048], P('expert', 'dp')
- grad_up_weight: bfloat16 [128, 768, 2048], P('expert', 'dp')
- grad_down_weight: bfloat16 [128, 768, 2048], P('expert', None, 'dp')
Inputs may be any that keep to these rules, and one draw needn't show every extreme that they name: `routes`: each row names 8 different experts. Among the rows of one device no expert is named more than 2 times, and in some device's rows some expert is named exactly 2 times.
All inputs are finite; a program needn't handle non-finite values.
Results may differ from a plain program's by a relative error of at most 0.0058.
Values may be sent and summed in bfloat16 or wider, within the bound.
A program may use at most 64 MiB of HBM per device.

v0:
```python
import jax
import jax.numpy as jnp
from jax import lax
from jax.sharding import PartitionSpec as P


def placement(routes, gate_values, experts, capacity):
    onehot = routes[:, :, None] == jnp.arange(experts, dtype=jnp.int32)[None, None, :]
    named = jnp.sum(onehot.astype(jnp.int32), axis=1)
    earlier = jnp.cumsum(named, axis=0) - named
    slot_ids = jnp.arange(capacity, dtype=jnp.int32)[None, :, None]
    placer = (named.T[:, None, :] == 1) & (earlier.T[:, None, :] == slot_ids)
    token_gate = jnp.sum(
        jnp.where(onehot, gate_values[:, :, None], jnp.zeros((), jnp.float32)), axis=1
    )
    slot_gate = jnp.sum(placer.astype(jnp.float32) * token_gate.T[:, None, :], axis=2)
    return (placer, slot_gate)


def body(tokens, cotangent, routes, gate_values, gate_weight, up_weight, down_weight):
    tok_rows = tokens.shape[0]
    width = tokens.shape[1]
    top_count = routes.shape[1]
    experts = lax.axis_size("expert")
    groups = lax.axis_size("dp")
    quarter = width // groups
    capacity = min(tok_rows, max(2, 2 * tok_rows * top_count // experts))
    placer, _ = placement(routes, gate_values, experts, capacity)
    row_input = jnp.einsum(
        "est,td->esd", placer.astype(jnp.bfloat16), tokens, preferred_element_type=jnp.float32
    ).astype(jnp.bfloat16)
    arrived_input = lax.all_to_all(row_input, "expert", split_axis=0, concat_axis=0, tiled=True)
    inputs_all = lax.all_gather(
        arrived_input.reshape(experts * capacity, width), "dp", axis=0, tiled=True
    )
    packed = jnp.concatenate(
        [cotangent.astype(jnp.float32), routes.astype(jnp.float32), gate_values], axis=1
    )
    col = lax.all_gather(packed, "dp", axis=0, tiled=False)
    col_routes = col[:, :, width : width + top_count].astype(jnp.int32)
    col_gates = col[:, :, width + top_count :]
    me = lax.axis_index("dp")
    cot_q = lax.dynamic_slice_in_dim(col[:, :, :width], me * quarter, quarter, axis=2).astype(
        jnp.bfloat16
    )
    col_placer, col_slot_gate = jax.vmap(lambda r, g: placement(r, g, experts, capacity))(
        col_routes, col_gates
    )
    picked_cot = jnp.einsum(
        "gest,gtd->egsd", col_placer.astype(jnp.bfloat16), cot_q, preferred_element_type=jnp.float32
    )
    row_cot = (jnp.transpose(col_slot_gate, (1, 0, 2))[:, :, :, None] * picked_cot).astype(
        jnp.bfloat16
    )
    arrived_cot = lax.all_to_all(row_cot, "expert", split_axis=0, concat_axis=0, tiled=True)
    cot_quarter = jnp.transpose(arrived_cot, (1, 0, 2, 3)).reshape(
        groups * experts * capacity, quarter
    )
    gate_local = gate_weight[0]
    up_local = up_weight[0]
    down_local = down_weight[0]
    contract_last = (((1,), (1,)), ((), ()))
    gate_pre = lax.dot_general(
        gate_local, inputs_all, contract_last, preferred_element_type=jnp.float32
    )
    up_pre = lax.dot_general(
        up_local, inputs_all, contract_last, preferred_element_type=jnp.float32
    )
    hidden_part = (jax.nn.silu(gate_pre) * up_pre).astype(jnp.bfloat16)
    hidden_all = lax.all_gather(hidden_part, "dp", axis=0, tiled=True)
    contract_lead = (((0,), (0,)), ((), ()))
    expert_out = lax.dot_general(
        hidden_all, down_local, contract_lead, preferred_element_type=jnp.float32
    ).astype(jnp.bfloat16)
    grad_down = jnp.dot(hidden_all, cot_quarter, preferred_element_type=jnp.float32).astype(
        jnp.bfloat16
    )
    grad_hidden = lax.psum_scatter(
        lax.dot_general(
            down_local, cot_quarter, contract_last, preferred_element_type=jnp.float32
        ).astype(jnp.bfloat16),
        "dp",
        scatter_dimension=0,
        tiled=True,
    ).astype(jnp.float32)
    sigma = jax.nn.sigmoid(gate_pre)
    grad_gate = (grad_hidden * up_pre * sigma * (1.0 + gate_pre * (1.0 - sigma))).astype(
        jnp.bfloat16
    )
    grad_up = (grad_hidden * jax.nn.silu(gate_pre)).astype(jnp.bfloat16)
    grad_gate_local = jnp.dot(grad_gate, inputs_all, preferred_element_type=jnp.float32).astype(
        jnp.bfloat16
    )
    grad_up_local = jnp.dot(grad_up, inputs_all, preferred_element_type=jnp.float32).astype(
        jnp.bfloat16
    )
    out_blocks = jnp.transpose(expert_out.reshape(groups, experts, capacity, quarter), (1, 0, 2, 3))
    returned = lax.all_to_all(out_blocks, "expert", split_axis=0, concat_axis=0, tiled=True)
    combine = col_placer.astype(jnp.float32) * col_slot_gate[:, :, :, None]
    mixed_q = jnp.einsum(
        "gest,egsd->gtd",
        combine,
        returned.astype(jnp.float32),
        precision=lax.Precision.HIGHEST,
        preferred_element_type=jnp.float32,
    ).astype(jnp.bfloat16)
    mixed = lax.all_to_all(mixed_q, "dp", split_axis=0, concat_axis=2, tiled=True)
    return (mixed[0], grad_gate_local[None], grad_up_local[None], grad_down[None])


def solution(mesh):
    in_specs = (
        P(("dp", "expert"), None),
        P(("dp", "expert"), None),
        P(("dp", "expert"), None),
        P(("dp", "expert"), None),
        P("expert", "dp", None),
        P("expert", "dp", None),
        P("expert", None, "dp"),
    )
    out_specs = (
        P(("dp", "expert"), None),
        P("expert", "dp", None),
        P("expert", "dp", None),
        P("expert", None, "dp"),
    )
    return jax.shard_map(body, mesh=mesh, in_specs=in_specs, out_specs=out_specs, check_vma=False)
```

profile of v0, /device:TPU:8, one launch (start us, length us, event | category | flops | bytes accessed | tf_op | source)
XLA Modules:
  0.0 215.8 jit_solution(4041124225692408910)
XLA Ops:
  7.2 0.8 copy.36
  8.2 1.3 convolution_convert_fusion
  9.5 1.1 copy.37
  10.6 48.6 %all_to_all.30 = bf16[128,2,2048]{2,1,0:T(2,128)(2,1)S(1)} all-to-all(bf16[128,2,2048]{2,1,0:T(2,128)(2,1)S(1)} %copy.37), channel_id=1, replica_groups=mesh['dp'=4,'expert'=128] {'expert'}, dimensions={0} | all-to-all | bytes 2097152 | tf_op jit(solution)/shard_map/all_to_all | solution.py:32
  59.2 1.2 reshape.30
  60.7 14.5 %all-gather = f32[64,2064]{1,0:T(8,128)S(1)} all-gather(f32[16,2064]{1,0:T(8,128)S(1)} %concatenate.3), channel_id=2, replica_groups=mesh['dp'=4,'expert'=128] {'dp'}, dimensions={0}, use_global_device_ids=true | all-gather | bytes 660480 | tf_op jit(solution)/shard_map/all_gather | solution.py:39
  76.4 2.1 copy.41
  78.4 5.3 %all-to-all-start.3 = ((bf16[128,4,2,512]{3,2,1,0:T(2,128)(2,1)}), bf16[128,4,2,512]{3,2,1,0:T(2,128)(2,1)S(1)}, u32[]{:S(2)}, u32[]{:S(2)}) async-start(bf16[128,4,2,512]{3,2,1,0:T(2,128)(2,1)} %copy.41), calls=%async_computation.3 | async-start | bytes 2097152 | tf_op jit(solution)/shard_map/all_to_all | solution.py:55
  83.8 24.2 %all-gather.4.cloned.1.call-done = bf16[1024,2048]{1,0:T(8,128)(2,1)} async-done(((bf16[256,2048]{1,0:T(8,128)(2,1)}), bf16[1024,2048]{1,0:T(8,128)(2,1)}) %all-gather.4.cloned.1.call-update) | async-done | bytes 4194320 | tf_op jit(solution)/shard_map/all_gather | solution.py:33
  108.0 3.9 %convolution_bitcast_fusion.1 = f32[192,1024]{1,0:T(8,128)S(1)} fusion(bf16[1024,2048]{1,0:T(8,128)(2,1)} %all-gather.4.cloned.1.call-done, bf16[1,192,2048]{2,1,0:T(8,128)(2,1)S(1)} %copy-done.8), kind=kOutput, calls=%fused_computation.13 | convolution fusion | flops 805306368 | bytes 5767168 | tf_op jit(solution)/shard_map/dot_general | solution.py:63
  111.9 4.1 %multiply_convert_fusion = (bf16[192,1024]{1,0:T(8,128)(2,1)}, f32[192,1024]{1,0:T(8,128)}) fusion(f32[192,1024]{1,0:T(8,128)S(1)} %convolution_bitcast_fusion.1, bf16[1024,2048]{1,0:T(8,128)(2,1)S(1)} %copy-done.6, bf16[1,192,2048]{2,1,0:T(8,128)(2,1)} %param.12), kind=kOutput, calls=%fused_computation.28 | convolution fusion | flops 806486016 | bytes 6946816 | tf_op jit(solution)/shard_map/dot_general | solution.py:66
  117.5 2.2 %fusion.3 = bf16[768,1024]{1,0:T(8,128)(2,1)} fusion(bf16[1024,512]{1,0:T(8,128)(2,1)S(1)} %reshape.32, bf16[1,768,512]{2,1,0:T(8,128)(2,1)S(1)} %copy-done), kind=kOutput, calls=%fused_computation.9 | convolution fusion | flops 806092800 | bytes 3407872 | tf_op jit(solution)/shard_map/dot_general | solution.py:79
  119.7 28.1 %all-gather.6.cloned.1.call-done = bf16[768,1024]{1,0:T(8,128)(2,1)} async-done(((bf16[192,1024]{1,0:T(8,128)(2,1)}), bf16[768,1024]{1,0:T(8,128)(2,1)}) %all-gather.6.cloned.1.call-update) | async-done | bytes 1572880 | tf_op jit(solution)/shard_map/all_gather | solution.py:70
  147.8 2.4 %convolution_convert_fusion.4 = bf16[1024,512]{1,0:T(8,128)(2,1)S(1)} fusion(bf16[768,1024]{1,0:T(8,128)(2,1)} %all-gather.6.cloned.1.call-done, bf16[1,768,512]{2,1,0:T(8,128)(2,1)S(1)} %copy-done), kind=kOutput, calls=%fused_computation.8 | convolution fusion | flops 805830656 | bytes 3407872 | tf_op jit(solution)/shard_map/dot_general | solution.py:72
  150.6 1.8 copy.51
  152.4 14.2 %all-to-all-start.1 = ((bf16[128,4,2,512]{3,2,1,0:T(2,128)(2,1)}), bf16[128,4,2,512]{3,2,1,0:T(2,128)(2,1)S(1)}, u32[]{:S(2)}, u32[]{:S(2)}) async-start(bf16[128,4,2,512]{3,2,1,0:T(2,128)(2,1)} %bitcast.70), calls=%async_computation.1 | async-start | bytes 2097152 | tf_op jit(solution)/shard_map/all_to_all | solution.py:98
  166.6 15.2 %reduce-scatter.2.cloned.1.call-done = bf16[192,1024]{1,0:T(8,128)(2,1)} async-done(((bf16[768,1024]{1,0:T(8,128)(2,1)}), bf16[192,1024]{1,0:T(8,128)(2,1)}) %reduce-scatter.2.cloned.1.call-update) | async-done | bytes 393232 | tf_op jit(solution)/shard_map/reduce_scatter | solution.py:78
  181.8 4.4 %fusion.1 = bf16[1,192,2048]{2,1,0:T(8,128)(2,1)} fusion(bf16[1024,2048]{1,0:T(8,128)(2,1)} %all-gather.4.cloned.1.call-done, bf16[192,1024]{1,0:T(8,128)(2,1)} %reduce-scatter.2.cloned.1.call-done, f32[192,1024]{1,0:T(8,128)S(1)} %copy-done.11), kind=kOutput, calls=%fused_computation.4 | convolution fusion | flops 807075840 | bytes 6160384 | tf_op jit(solution)/shard_map/dot_general | solution.py:94
  186.2 2.0 fusion
  188.3 9.8 %all-to-all-done.1 = bf16[128,4,2,512]{3,2,1,0:T(2,128)(2,1)S(1)} async-done(((bf16[128,4,2,512]{3,2,1,0:T(2,128)(2,1)}), bf16[128,4,2,512]{3,2,1,0:T(2,128)(2,1)S(1)}, u32[]{:S(2)}, u32[]{:S(2)}) %all-to-all-start.1) | async-done | bytes 1048608 | tf_op jit(solution)/shard_map/all_to_all | solution.py:98
  198.0 1.6 fusion.5
  199.7 3.3 %all-to-all-start.2 = ((bf16[4,16,512]{2,1,0:T(8,128)(2,1)}), bf16[4,16,512]{2,1,0:T(8,128)(2,1)S(1)}, u32[]{:S(2)}, u32[]{:S(2)}) async-start(bf16[4,16,512]{2,1,0:T(8,128)(2,1)} %fusion.5), calls=%async_computation.2 | async-start | bytes 131072 | tf_op jit(solution)/shard_map/all_to_all | solution.py:107
  203.0 3.3 %fusion.4 = bf16[1,768,512]{2,1,0:T(8,128)(2,1)} fusion(bf16[768,1024]{1,0:T(8,128)(2,1)} %all-gather.6.cloned.1.call-done, bf16[1024,512]{1,0:T(8,128)(2,1)S(1)} %copy-done.2), kind=kOutput, calls=%fused_computation.11 | convolution fusion | flops 805699584 | bytes 3407872 | tf_op jit(solution)/shard_map/dot_general | solution.py:75
  206.3 2.3 %all-to-all-done.2 = bf16[4,16,512]{2,1,0:T(8,128)(2,1)S(1)} async-done(((bf16[4,16,512]{2,1,0:T(8,128)(2,1)}), bf16[4,16,512]{2,1,0:T(8,128)(2,1)S(1)}, u32[]{:S(2)}, u32[]{:S(2)}) %all-to-all-start.2) | async-done | bytes 65568 | tf_op jit(solution)/shard_map/all_to_all | solution.py:107
  (57 shorter events, 4.1 us)
Async XLA Ops:
  7.2 110.3 %copy-start = (bf16[1,768,512]{2,1,0:T(8,128)(2,1)S(1)}, bf16[1,768,512]{2,1,0:T(8,128)(2,1)}, u32[]{:S(2)}) copy-start(bf16[1,768,512]{2,1,0:T(8,128)(2,1)} %param.13) | copy-start | bytes 2359300
  7.2 100.8 %all-gather.4.cloned.1.call-start = ((), (), s32[]{:S(2)}) async-start(), calls=%async_computation.5 | async-start | bytes 5242880 | tf_op jit(solution)/shard_map/all_gather | solution.py:33
  59.2 1.3 copy-start.4
  59.2 1.3 copy-start.5
  59.2 1.4 copy-start.3
  76.4 31.7 %copy-start.8 = (bf16[1,192,2048]{2,1,0:T(8,128)(2,1)S(1)}, bf16[1,192,2048]{2,1,0:T(8,128)(2,1)}, u32[]{:S(2)}) copy-start(bf16[1,192,2048]{2,1,0:T(8,128)(2,1)} %param.11) | copy-start | bytes 2359300
  78.4 37.8 %all-to-all-start.3 = ((bf16[128,4,2,512]{3,2,1,0:T(2,128)(2,1)}), bf16[128,4,2,512]{3,2,1,0:T(2,128)(2,1)S(1)}, u32[]{:S(2)}, u32[]{:S(2)}) async-start(bf16[128,4,2,512]{3,2,1,0:T(2,128)(2,1)} %copy.41), calls=%async_computation.3 | async-start | bytes 2097152 | tf_op jit(solution)/shard_map/all_to_all | solution.py:55
  83.8 64.0 %all-gather.6.cloned.1.call-start = ((), (), s32[]{:S(2)}) async-start(), calls=%async_computation.6 | async-start | bytes 1966080 | tf_op jit(solution)/shard_map/all_gather | solution.py:70
  108.0 3.9 %copy-start.6 = (bf16[1024,2048]{1,0:T(8,128)(2,1)S(1)}, bf16[1024,2048]{1,0:T(8,128)(2,1)}, u32[]{:S(2)}) copy-start(bf16[1024,2048]{1,0:T(8,128)(2,1)} %all-gather.4.cloned.1.call-done) | copy-start | bytes 12582916
  111.9 4.1 %copy-start.10 = (f32[192,1024]{1,0:T(8,128)}, f32[192,1024]{1,0:T(8,128)S(1)}, u32[]{:S(2)}) copy-start(f32[192,1024]{1,0:T(8,128)S(1)} %convolution_bitcast_fusion.1) | copy-start | bytes 2359300
  116.0 65.7 %reduce-scatter.2.cloned.1.call-start = ((), (), s32[]{:S(2)}) async-start(), calls=%async_computation.7 | async-start | bytes 1966080 | tf_op jit(solution)/shard_map/reduce_scatter | solution.py:78
  117.5 2.2 %copy-start.1 = (bf16[1024,512]{1,0:T(8,128)(2,1)}, bf16[1024,512]{1,0:T(8,128)(2,1)S(1)}, u32[]{:S(2)}) copy-start(bf16[1024,512]{1,0:T(8,128)(2,1)S(1)} %reshape.32) | copy-start | bytes 3145732
  150.6 31.2 %copy-start.11 = (f32[192,1024]{1,0:T(8,128)S(1)}, f32[192,1024]{1,0:T(8,128)}, u32[]{:S(2)}) copy-start(f32[192,1024]{1,0:T(8,128)} %copy-done.10) | copy-start | bytes 2359300
  152.4 45.6 %all-to-all-start.1 = ((bf16[128,4,2,512]{3,2,1,0:T(2,128)(2,1)}), bf16[128,4,2,512]{3,2,1,0:T(2,128)(2,1)S(1)}, u32[]{:S(2)}, u32[]{:S(2)}) async-start(bf16[128,4,2,512]{3,2,1,0:T(2,128)(2,1)} %bitcast.70), calls=%async_computation.1 | async-start | bytes 2097152 | tf_op jit(solution)/shard_map/all_to_all | solution.py:98
  181.8 4.4 %copy-start.7 = (bf16[1024,2048]{1,0:T(8,128)(2,1)S(1)}, bf16[1024,2048]{1,0:T(8,128)(2,1)}, u32[]{:S(2)}) copy-start(bf16[1024,2048]{1,0:T(8,128)(2,1)} %all-gather.4.cloned.1.call-done) | copy-start | bytes 12582916
  181.8 4.4 %copy-start.9 = (bf16[192,1024]{1,0:T(8,128)(2,1)S(1)}, bf16[192,1024]{1,0:T(8,128)(2,1)}, u32[]{:S(2)}) copy-start(bf16[192,1024]{1,0:T(8,128)(2,1)} %reduce-scatter.2.cloned.1.call-done) | copy-start | bytes 1179652
  181.8 4.4 %copy-start.12 = (f32[192,1024]{1,0:T(8,128)S(1)}, f32[192,1024]{1,0:T(8,128)}, u32[]{:S(2)}) copy-start(f32[192,1024]{1,0:T(8,128)} %copy-done.10) | copy-start | bytes 2359300
  181.8 4.4 %copy-start.13 = (f32[192,1024]{1,0:T(8,128)S(1)}, f32[192,1024]{1,0:T(8,128)}, u32[]{:S(2)}) copy-start(f32[192,1024]{1,0:T(8,128)} %get-tuple-element.7) | copy-start | bytes 2359300
  186.2 16.8 %copy-start.2 = (bf16[1024,512]{1,0:T(8,128)(2,1)S(1)}, bf16[1024,512]{1,0:T(8,128)(2,1)}, u32[]{:S(2)}) copy-start(bf16[1024,512]{1,0:T(8,128)(2,1)} %copy-done.1) | copy-start | bytes 3145732
  199.7 8.9 %all-to-all-start.2 = ((bf16[4,16,512]{2,1,0:T(8,128)(2,1)}), bf16[4,16,512]{2,1,0:T(8,128)(2,1)S(1)}, u32[]{:S(2)}, u32[]{:S(2)}) async-start(bf16[4,16,512]{2,1,0:T(8,128)(2,1)} %fusion.5), calls=%async_computation.2 | async-start | bytes 131072 | tf_op jit(solution)/shard_map/all_to_all | solution.py:107
Sparse Core Ops, SparseCore 0:
  60.6 47.3 all-gather.3
  116.2 31.5 all-gather.5
  150.6 31.1 reduce-scatter.1
where the time goes:
time: 216 us
  waiting for transfers between devices  79.6 us (37%)
  blocking collectives  63.1 us (29%)
  matrix products  25.7 us (12%)
  starting transfers between devices  23.1 us (11%)
  between operations  14 us (6%)
  local copies, waits for them, and re-layouts  9.6 us (4%)
    all_to_all x1, blocking collectives, body(): lax.all_to_all(row_input, 'expert', split_axis=0, concat_axis=0, tiled=True)  48.6 us
    all_gather x1, waiting for transfers between devices, body(): hidden_all = lax.all_gather(hidden_part, 'dp', axis=0, tiled=True)  28.1 us
    all_gather x1, waiting for transfers between devices, body(): lax.all_gather(arrived_input.reshape(experts * capacity, width), 'dp', ax...  24.2 us
    reduce_scatter x1, waiting for transfers between devices, body(): lax.psum_scatter(lax.dot_general(down_local, cot_quarter, contract_last,...  15.2 us
    all_gather x1, blocking collectives, body(): col = lax.all_gather(packed, 'dp', axis=0, tiled=False)  14.5 us
    all_to_all x1, starting transfers between devices, body(): lax.all_to_all(out_blocks, 'expert', split_axis=0, concat_axis=0, tiled=T...  14.2 us
    all_to_all x1, waiting for transfers between devices, body(): lax.all_to_all(out_blocks, 'expert', split_axis=0, concat_axis=0, tiled=T...  9.77 us
    all_to_all x1, starting transfers between devices, body(): lax.all_to_all(row_cot, 'expert', split_axis=0, concat_axis=0, tiled=True)  5.32 us
  transfers between devices with their start and end apart: 6, of which 5 were waited for; matrix products, arithmetic and copies ran while one was open for 13% of the time, Pallas kernels for 0%

commit v1 on v0

--- a/solution.py
+++ b/solution.py
@@ -67,7 +67,21 @@
         up_local, inputs_all, contract_last, preferred_element_type=jnp.float32
     )
     hidden_part = (jax.nn.silu(gate_pre) * up_pre).astype(jnp.bfloat16)
-    hidden_all = lax.all_gather(hidden_part, "dp", axis=0, tiled=True)
+    ways, here, lap = (lax.axis_size("dp"), lax.axis_index("dp"), hidden_part.shape[0])
+    dims = [n * ways if d == 0 else n for d, n in enumerate(hidden_part.shape)]
+    full = lax.dynamic_update_slice_in_dim(
+        jnp.zeros(dims, hidden_part.dtype), hidden_part, here * lap, axis=0
+    )
+    going_up = going_down = hidden_part
+    for far in range(1, ways // 2 + 1):
+        going_up = lax.ppermute(going_up, "dp", [(d, (d + 1) % ways) for d in range(ways)])
+        full = lax.dynamic_update_slice_in_dim(full, going_up, (here - far) % ways * lap, axis=0)
+        if 2 * far < ways:
+            going_down = lax.ppermute(going_down, "dp", [(d, (d - 1) % ways) for d in range(ways)])
+            full = lax.dynamic_update_slice_in_dim(
+                full, going_down, (here + far) % ways * lap, axis=0
+            )
+    hidden_all = full
     contract_lead = (((0,), (0,)), ((), ()))
     expert_out = lax.dot_general(
         hidden_all, down_local, contract_lead, preferred_element_type=jnp.float32

time: 216 us -> 225 us (1.042)
  local copies, waits for them, and re-layouts: 9.6 us -> 14.1 us
  waiting for transfers between devices: 79.6 us -> 83.7 us
    all_to_all x1, waiting for transfers between devices: 0.01 us -> 30.9 us  [body(): lax.all_to_all(row_cot, 'expert', split_axis=0, concat_axis=0, tiled=True)]
    all_gather x1 -> x0, waiting for transfers between devices: 28.1 us -> none  [body(): hidden_all = lax.all_gather(hidden_part, 'dp', axis=0, tiled=True)]
    ppermute x0 -> x3, waiting for transfers between devices: none -> 25.5 us  [the longest x2 25.5 us: body(): lax.ppermute(going_up, 'dp', [(d, (d + 1) % ways) for d in range(ways)])]
    all_gather x1, waiting for transfers between devices: 24.2 us -> 0.02 us  [body(): lax.all_gather(arrived_input.reshape(experts * capacity, width), 'dp', ax...]
    reduce_scatter x1, waiting for transfers between devices: 15.2 us -> 0.02 us  [body(): lax.psum_scatter(lax.dot_general(down_local, cot_quarter, contract_last,...]
    all_to_all x1, waiting for transfers between devices: 9.77 us -> 24.7 us  [body(): lax.all_to_all(out_blocks, 'expert', split_axis=0, concat_axis=0, tiled=T...]
    ppermute x0 -> x3, starting transfers between devices: none -> 9.13 us  [the longest x2 5.63 us: body(): lax.ppermute(going_up, 'dp', [(d, (d + 1) % ways) for d in range(ways)])]
    all_to_all x1, starting transfers between devices: 14.2 us -> 6.46 us  [body(): lax.all_to_all(out_blocks, 'expert', split_axis=0, concat_axis=0, tiled=T...]
  transfers between devices with their start and end apart: 6 -> 8, of which waited for: 5 -> 5; matrix products, arithmetic and copies ran while one was open for 13% -> 13% of each run, Pallas kernels for 0% -> 0%
where the time goes in v1:
time: 225 us; the launch traced here: 224 us
  waiting for transfers between devices  83.7 us (37%)
  blocking collectives  63.2 us (28%)
  starting transfers between devices  24.3 us (11%)
  matrix products  23.8 us (11%)
  between operations  14.4 us (6%)
  local copies, waits for them, and re-layouts  14.1 us (6%)
    all_to_all x1, blocking collectives, body(): lax.all_to_all(row_input, 'expert', split_axis=0, concat_axis=0, tiled=True)  48.6 us
    all_to_all x1, waiting for transfers between devices, body(): lax.all_to_all(row_cot, 'expert', split_axis=0, concat_axis=0, tiled=True)  30.9 us
    ppermute x2, waiting for transfers between devices, body(): lax.ppermute(going_up, 'dp', [(d, (d + 1) % ways) for d in range(ways)])  25.5 us
    all_to_all x1, waiting for transfers between devices, body(): lax.all_to_all(out_blocks, 'expert', split_axis=0, concat_axis=0, tiled=T...  24.7 us
    all_gather x1, blocking collectives, body(): col = lax.all_gather(packed, 'dp', axis=0, tiled=False)  14.5 us
    all_to_all x1, starting transfers between devices, body(): lax.all_to_all(out_blocks, 'expert', split_axis=0, concat_axis=0, tiled=T...  6.46 us
    ppermute x2, starting transfers between devices, body(): lax.ppermute(going_up, 'dp', [(d, (d + 1) % ways) for d in range(ways)])  5.63 us
    all_to_all x1, starting transfers between devices, body(): lax.all_to_all(row_cot, 'expert', split_axis=0, concat_axis=0, tiled=True)  5.32 us
  transfers between devices with their start and end apart: 8, of which 5 were waited for; matrix products, arithmetic and copies ran while one was open for 13% of the time, Pallas kernels for 0%

profile of v1, /device:TPU:8, one launch (start us, length us, event | category | flops | bytes accessed | tf_op | source)
XLA Modules:
  0.0 224.1 jit_solution(12196098250368525339)
XLA Ops:
  10.6 48.6 %all_to_all.30 = bf16[128,2,2048]{2,1,0:T(2,128)(2,1)S(1)} all-to-all(bf16[128,2,2048]{2,1,0:T(2,128)(2,1)S(1)} %copy.37), channel_id=1, replica_groups=mesh['dp'=4,'expert'=128] {'expert'}, dimensions={0} | all-to-all | bytes 2097152 | tf_op jit(solution)/shard_map/all_to_all | solution.py:32
  60.7 14.5 %all-gather = f32[64,2064]{1,0:T(8,128)S(1)} all-gather(f32[16,2064]{1,0:T(8,128)S(1)} %concatenate.3), channel_id=2, replica_groups=mesh['dp'=4,'expert'=128] {'dp'}, dimensions={0}, use_global_device_ids=true | all-gather | bytes 660480 | tf_op jit(solution)/shard_map/all_gather | solution.py:39
  76.4 2.1 copy.41
  78.4 5.3 %all-to-all-start.3 = ((bf16[128,4,2,512]{3,2,1,0:T(2,128)(2,1)}), bf16[128,4,2,512]{3,2,1,0:T(2,128)(2,1)S(1)}, u32[]{:S(2)}, u32[]{:S(2)}) async-start(bf16[128,4,2,512]{3,2,1,0:T(2,128)(2,1)} %copy.41), calls=%async_computation.3 | async-start | bytes 2097152 | tf_op jit(solution)/shard_map/all_to_all | solution.py:55
  83.8 30.9 %all-to-all-done.3 = bf16[128,4,2,512]{3,2,1,0:T(2,128)(2,1)S(1)} async-done(((bf16[128,4,2,512]{3,2,1,0:T(2,128)(2,1)}), bf16[128,4,2,512]{3,2,1,0:T(2,128)(2,1)S(1)}, u32[]{:S(2)}, u32[]{:S(2)}) %all-to-all-start.3) | async-done | bytes 1048608 | tf_op jit(solution)/shard_map/all_to_all | solution.py:55
  115.9 2.2 fusion.3
  119.2 3.9 %convolution_bitcast_fusion.1 = f32[192,1024]{1,0:T(8,128)S(1)} fusion(bf16[1024,2048]{1,0:T(8,128)(2,1)} %all-gather.3.cloned.1.call-done, bf16[1,192,2048]{2,1,0:T(8,128)(2,1)S(1)} %copy-done.7), kind=kOutput, calls=%fused_computation.13 | convolution fusion | flops 805306368 | bytes 5767168 | tf_op jit(solution)/shard_map/dot_general | solution.py:63
  124.5 2.6 %constant_dynamic-update-slice_fusion.3 = (bf16[768,1024]{1,0:T(8,128)(2,1)S(1)}, bf16[192,1024]{1,0:T(8,128)(2,1)}, f32[192,1024]{1,0:T(8,128)}) fusion(bf16[768,1024]{1,0:T(8,128)(2,1)S(1)} %broadcast_in_dim.22, s32[]{:T(128)S(6)} %select_n.35, f32[192,1024]{1,0:T(8,128)S(1)} %convolution_bitcast_fusion.1, bf16[1024,2048]{1,0:T(8,128)(2,1)S(1)} %copy-done.5, ...), kind=kOutput, calls=%fused_computation.63 | convolution fusion | flops 806486016 | bytes 7340036 | tf_op jit(solution)/shard_map/dot_general | solution.py:66
  127.1 3.5 %collective-permute-start = (bf16[192,1024]{1,0:T(8,128)(2,1)}, bf16[192,1024]{1,0:T(8,128)(2,1)S(1)}, u32[]{:S(2)}, u32[]{:S(2)}) collective-permute-start(bf16[192,1024]{1,0:T(8,128)(2,1)} %get-tuple-element.5), channel_id=1, source_target_pairs={{0,128},{128,256},{256,384},{384,0},{1,129},{129,257},{257,385},{3... | collective-permute-start | bytes 1179656 | tf_op jit(solution)/shard_map/ppermute | solution.py:77
  130.7 3.5 %collective-permute-start.1 = (bf16[192,1024]{1,0:T(8,128)(2,1)}, bf16[192,1024]{1,0:T(8,128)(2,1)}, u32[]{:S(2)}, u32[]{:S(2)}) collective-permute-start(bf16[192,1024]{1,0:T(8,128)(2,1)} %get-tuple-element.5), channel_id=1, source_target_pairs={{0,384},{128,0},{256,128},{384,256},{1,385},{129,1},{257,129},{385... | collective-permute-start | bytes 1179656 | tf_op jit(solution)/shard_map/ppermute | solution.py:80
  134.2 15.1 %collective-permute-done = bf16[192,1024]{1,0:T(8,128)(2,1)S(1)} collective-permute-done((bf16[192,1024]{1,0:T(8,128)(2,1)}, bf16[192,1024]{1,0:T(8,128)(2,1)S(1)}, u32[]{:S(2)}, u32[]{:S(2)}) %collective-permute-start) | collective-permute-done | bytes 393248 | tf_op jit(solution)/shard_map/ppermute | solution.py:77
  149.3 2.1 collective-permute-start.2
  152.6 10.3 %collective-permute-done.2 = bf16[192,1024]{1,0:T(8,128)(2,1)S(1)} collective-permute-done((bf16[192,1024]{1,0:T(8,128)(2,1)S(1)}, bf16[192,1024]{1,0:T(8,128)(2,1)S(1)}, u32[]{:S(2)}, u32[]{:S(2)}) %collective-permute-start.2) | collective-permute-done | bytes 393248 | tf_op jit(solution)/shard_map/ppermute | solution.py:77
  163.0 2.0 convolution_convert_fusion.4
  165.0 1.5 reshape.31
  166.4 1.7 copy.51
  168.1 6.5 %all-to-all-start.1 = ((bf16[128,4,2,512]{3,2,1,0:T(2,128)(2,1)}), bf16[128,4,2,512]{3,2,1,0:T(2,128)(2,1)S(1)}, u32[]{:S(2)}, u32[]{:S(2)}) async-start(bf16[128,4,2,512]{3,2,1,0:T(2,128)(2,1)} %bitcast.70), calls=%async_computation.1 | async-start | bytes 2097152 | tf_op jit(solution)/shard_map/all_to_all | solution.py:112
  174.7 4.6 %fusion.1 = bf16[1,192,2048]{2,1,0:T(8,128)(2,1)} fusion(bf16[1024,2048]{1,0:T(8,128)(2,1)} %all-gather.3.cloned.1.call-done, bf16[192,1024]{1,0:T(8,128)(2,1)} %reduce-scatter.2.cloned.1.call-done, f32[192,1024]{1,0:T(8,128)} %copy-done.10), kind=kOutput, calls=%fused_computation.4 | convolution fusion | flops 807075840 | bytes 6160384 | tf_op jit(solution)/shard_map/dot_general | solution.py:108
  179.3 2.0 fusion
  181.3 24.7 %all-to-all-done.1 = bf16[128,4,2,512]{3,2,1,0:T(2,128)(2,1)S(1)} async-done(((bf16[128,4,2,512]{3,2,1,0:T(2,128)(2,1)}), bf16[128,4,2,512]{3,2,1,0:T(2,128)(2,1)S(1)}, u32[]{:S(2)}, u32[]{:S(2)}) %all-to-all-start.1) | async-done | bytes 1048608 | tf_op jit(solution)/shard_map/all_to_all | solution.py:112
  206.1 1.6 fusion.5
  207.7 3.3 %all-to-all-start.2 = ((bf16[4,16,512]{2,1,0:T(8,128)(2,1)}), bf16[4,16,512]{2,1,0:T(8,128)(2,1)S(1)}, u32[]{:S(2)}, u32[]{:S(2)}) async-start(bf16[4,16,512]{2,1,0:T(8,128)(2,1)} %fusion.5), calls=%async_computation.2 | async-start | bytes 131072 | tf_op jit(solution)/shard_map/all_to_all | solution.py:121
  211.0 3.1 %fusion.4 = bf16[1,768,512]{2,1,0:T(8,128)(2,1)} fusion(bf16[768,1024]{1,0:T(8,128)(2,1)S(1)} %constant_dynamic-update-slice_fusion, bf16[1024,512]{1,0:T(8,128)(2,1)} %copy-done.1), kind=kOutput, calls=%fused_computation.11 | convolution fusion | flops 805699584 | bytes 3407872 | tf_op jit(solution)/shard_map/dot_general | solution.py:89
  214.1 2.5 %all-to-all-done.2 = bf16[4,16,512]{2,1,0:T(8,128)(2,1)S(1)} async-done(((bf16[4,16,512]{2,1,0:T(8,128)(2,1)}), bf16[4,16,512]{2,1,0:T(8,128)(2,1)S(1)}, u32[]{:S(2)}, u32[]{:S(2)}) %all-to-all-start.2) | async-done | bytes 65568 | tf_op jit(solution)/shard_map/all_to_all | solution.py:121
  (62 shorter events, 11.5 us)
Async XLA Ops:
  7.2 108.7 %copy-start = (bf16[1,768,512]{2,1,0:T(8,128)(2,1)S(1)}, bf16[1,768,512]{2,1,0:T(8,128)(2,1)}, u32[]{:S(2)}) copy-start(bf16[1,768,512]{2,1,0:T(8,128)(2,1)} %param.13) | copy-start | bytes 2359300
  7.2 111.0 %all-gather.3.cloned.1.call-start = ((), (), s32[]{:S(2)}) async-start(), calls=%async_computation.5 | async-start | bytes 5242880 | tf_op jit(solution)/shard_map/all_gather | solution.py:33
  59.2 1.2 copy-start.3
  59.2 1.3 copy-start.4
  59.2 1.4 copy-start.2
  78.4 36.3 %all-to-all-start.3 = ((bf16[128,4,2,512]{3,2,1,0:T(2,128)(2,1)}), bf16[128,4,2,512]{3,2,1,0:T(2,128)(2,1)S(1)}, u32[]{:S(2)}, u32[]{:S(2)}) async-start(bf16[128,4,2,512]{3,2,1,0:T(2,128)(2,1)} %copy.41), calls=%async_computation.3 | async-start | bytes 2097152 | tf_op jit(solution)/shard_map/all_to_all | solution.py:55
  83.8 90.8 %reduce-scatter.2.cloned.1.call-start = ((), (), s32[]{:S(2)}) async-start(), calls=%async_computation.6 | async-start | bytes 1966080 | tf_op jit(solution)/shard_map/reduce_scatter | solution.py:92
  115.9 2.2 copy-start.1
  118.1 1.1 copy-start.7
  119.2 4.1 %copy-start.5 = (bf16[1024,2048]{1,0:T(8,128)(2,1)S(1)}, bf16[1024,2048]{1,0:T(8,128)(2,1)}, u32[]{:S(2)}) copy-start(bf16[1024,2048]{1,0:T(8,128)(2,1)} %all-gather.3.cloned.1.call-done) | copy-start | bytes 12582916
  123.1 4.0 %copy-start.10 = (f32[192,1024]{1,0:T(8,128)}, f32[192,1024]{1,0:T(8,128)S(1)}, u32[]{:S(2)}) copy-start(f32[192,1024]{1,0:T(8,128)S(1)} %convolution_bitcast_fusion.1) | copy-start | bytes 2359300
  123.1 1.4 copy-start.8
  127.1 22.2 %collective-permute-start = (bf16[192,1024]{1,0:T(8,128)(2,1)}, bf16[192,1024]{1,0:T(8,128)(2,1)S(1)}, u32[]{:S(2)}, u32[]{:S(2)}) collective-permute-start(bf16[192,1024]{1,0:T(8,128)(2,1)} %get-tuple-element.5), channel_id=1, source_target_pairs={{0,128},{128,256},{256,384},{384,0},{1,129},{129,257},{257,385},{3... | collective-permute-start | bytes 1179656 | tf_op jit(solution)/shard_map/ppermute | solution.py:77
  130.7 20.9 %collective-permute-start.1 = (bf16[192,1024]{1,0:T(8,128)(2,1)}, bf16[192,1024]{1,0:T(8,128)(2,1)}, u32[]{:S(2)}, u32[]{:S(2)}) collective-permute-start(bf16[192,1024]{1,0:T(8,128)(2,1)} %get-tuple-element.5), channel_id=1, source_target_pairs={{0,384},{128,0},{256,128},{384,256},{1,385},{129,1},{257,129},{385... | collective-permute-start | bytes 1179656 | tf_op jit(solution)/shard_map/ppermute | solution.py:80
  149.3 13.6 %collective-permute-start.2 = (bf16[192,1024]{1,0:T(8,128)(2,1)S(1)}, bf16[192,1024]{1,0:T(8,128)(2,1)S(1)}, u32[]{:S(2)}, u32[]{:S(2)}) collective-permute-start(bf16[192,1024]{1,0:T(8,128)(2,1)S(1)} %collective-permute-done), channel_id=1, source_target_pairs={{0,128},{128,256},{256,384},{384,0},{1,129},{129,257},{257,385},{3... | collective-permute-start | bytes 1179656 | tf_op jit(solution)/shard_map/ppermute | solution.py:77
  168.1 37.9 %all-to-all-start.1 = ((bf16[128,4,2,512]{3,2,1,0:T(2,128)(2,1)}), bf16[128,4,2,512]{3,2,1,0:T(2,128)(2,1)S(1)}, u32[]{:S(2)}, u32[]{:S(2)}) async-start(bf16[128,4,2,512]{3,2,1,0:T(2,128)(2,1)} %bitcast.70), calls=%async_computation.1 | async-start | bytes 2097152 | tf_op jit(solution)/shard_map/all_to_all | solution.py:112
  174.6 4.7 %copy-start.6 = (bf16[1024,2048]{1,0:T(8,128)(2,1)S(1)}, bf16[1024,2048]{1,0:T(8,128)(2,1)}, u32[]{:S(2)}) copy-start(bf16[1024,2048]{1,0:T(8,128)(2,1)} %all-gather.3.cloned.1.call-done) | copy-start | bytes 12582916
  174.6 4.6 %copy-start.9 = (bf16[192,1024]{1,0:T(8,128)(2,1)S(1)}, bf16[192,1024]{1,0:T(8,128)(2,1)}, u32[]{:S(2)}) copy-start(bf16[192,1024]{1,0:T(8,128)(2,1)} %reduce-scatter.2.cloned.1.call-done) | copy-start | bytes 1179652
  174.6 4.6 %copy-start.11 = (f32[192,1024]{1,0:T(8,128)S(1)}, f32[192,1024]{1,0:T(8,128)}, u32[]{:S(2)}) copy-start(f32[192,1024]{1,0:T(8,128)} %copy-done.10) | copy-start | bytes 2359300
  174.7 4.6 %copy-start.12 = (f32[192,1024]{1,0:T(8,128)S(1)}, f32[192,1024]{1,0:T(8,128)}, u32[]{:S(2)}) copy-start(f32[192,1024]{1,0:T(8,128)} %get-tuple-element.8) | copy-start | bytes 2359300
  207.7 8.9 %all-to-all-start.2 = ((bf16[4,16,512]{2,1,0:T(8,128)(2,1)}), bf16[4,16,512]{2,1,0:T(8,128)(2,1)S(1)}, u32[]{:S(2)}, u32[]{:S(2)}) async-start(bf16[4,16,512]{2,1,0:T(8,128)(2,1)} %fusion.5), calls=%async_computation.2 | async-start | bytes 131072 | tf_op jit(solution)/shard_map/all_to_all | solution.py:121
Sparse Core Ops, SparseCore 0:
  60.6 47.3 all-gather.2
  118.2 31.6 reduce-scatter.1
